TPU v7x, 32 devices: a whole 2x2x4 slice. The times are simulated.
32 devices in a mesh: ctx: 8 (over z, y), exp: 4 (over x, core).
Axes of the slice: x: 2, y: 2, z: 4, core: 2. Of those that a mesh axis runs over, the one named last changes fastest.
Arguments:
- queries: bfloat16 [1024, 4096], P('ctx', 'exp'), may hold values from -0.5 to 0.5
- attn_keys: bfloat16 [1024, 4096], P('ctx', 'exp'), may hold values from -0.5 to 0.5
- attn_values: bfloat16 [1024, 4096], P('ctx', 'exp'), may hold values from -3 to 3
- out_grad: bfloat16 [1024, 4096], P('ctx', 'exp'), may hold values from -0.75 to 0.75
- log_decay: float32 [1024, 32], P('ctx', 'exp'), may hold values from -1 to 0
- moe_input: bfloat16 [1024, 3072], P(('ctx', 'exp')), may hold values from -6 to 6
- routes: int32 [1024, 2], P(('ctx', 'exp')), may hold values from 0 to 7, all different within a row; in each aligned block of 32 rows (0 to 31, 32 to 63, ...) at most 16 rows name the same one
- route_weight: float32 [1024, 2], P(('ctx', 'exp')), may hold values from 0.25 to 1
- w_gate: bfloat16 [8, 9216, 3072], P('exp', 'ctx'), may hold values from -0.109375 to 0.109375
- w_up: bfloat16 [8, 9216, 3072], P('exp', 'ctx'), may hold values from -0.109375 to 0.109375
- w_down: bfloat16 [8, 9216, 3072], P('exp', 'ctx'), may hold values from -0.0625 to 0.0625
Outputs:
- attn_out: bfloat16 [1024, 4096], P('ctx', 'exp')
- grad_q: bfloat16 [1024, 4096], P('ctx', 'exp')
- grad_k: bfloat16 [1024, 4096], P('ctx', 'exp')
- derivative_wrt_entries: bfloat16 [1024, 4096], P('ctx', 'exp')
- moe_out: bfloat16 [1024, 3072], P(('ctx', 'exp'))
Inputs may be any that keep to these rules, and one draw needn't show every extreme that they name: `routes`: in the rows of one device no expert is named more than 16 times; each row names two different experts.
All inputs are finite; a program needn't handle non-finite values.
Results may differ from a plain program's by a relative error of at most 0.025.
Values may be sent and summed in bfloat16 or wider, within the bound.
No kernel may reach another device: no remote copies, remote signals or barrier semaphores. Data moves between devices by JAX's collectives and lax.ppermute only.
A program may use at most 128 MiB of HBM per device.

v0:
```python
import jax
import jax.numpy as jnp
from jax import lax
from jax.sharding import PartitionSpec as P


def entering(value, axis, combine, identity, reverse):
    length, position = (lax.axis_size(axis), lax.axis_index(axis))
    everything = jax.tree.map(
        lambda part, kind: lax.all_gather(part.astype(kind), axis),
        value,
        (jnp.bfloat16, jnp.bfloat16),
    )
    start = jax.tree.map(
        lambda part, zero: jnp.broadcast_to(jnp.asarray(zero, part.dtype), part.shape),
        value,
        identity,
    )

    def step(k, before):
        at = length - 1 - k if reverse else k
        reached = at > position if reverse else at < position
        new = combine(
            before, jax.tree.map(lambda part, own: part[at].astype(own.dtype), everything, value)
        )
        return jax.tree.map(lambda a, b: jnp.where(reached, a, b), new, before)

    return lax.fori_loop(0, length, step, start)


def chain_combine(earlier, later):
    return (earlier[0] * later[0], later[0][:, None, None] * earlier[1] + later[1])


def attention(queries, attn_keys, attn_values, out_grad, log_decay):
    length = queries.shape[0]
    heads = log_decay.shape[1]
    width = queries.shape[1] // heads
    shaped = (length, heads, width)
    q_heads = queries.reshape(shaped)
    k_heads = attn_keys.reshape(shaped)
    v_heads = attn_values.reshape(shaped)
    gradient_heads = out_grad.reshape(shaped)
    cum_decay = jnp.cumsum(log_decay, axis=0)
    total = cum_decay[length - 1]
    position = jnp.arange(length, dtype=jnp.int32)
    causal = (position[:, None] >= position[None, :])[None]
    spread = cum_decay.T[:, :, None] - cum_decay.T[:, None, :]
    block_weight = jnp.where(causal, jnp.exp(jnp.where(causal, spread, 0.0)), 0.0)
    rising_edge = jnp.exp(cum_decay)[:, :, None]
    falling_edge = jnp.exp(total[None, :] - cum_decay)[:, :, None]
    scaled_queries = q_heads.astype(jnp.float32) * rising_edge
    full_keys = k_heads.astype(jnp.float32)
    full_values = v_heads.astype(jnp.float32)
    scaled_gradient = gradient_heads.astype(jnp.float32) * rising_edge
    running_block_state = jnp.einsum(
        "mly,mlf->lyf", full_keys * falling_edge, full_values, precision=lax.Precision.HIGHEST
    )
    state_gradient = jnp.einsum(
        "nbd,nbw->bdw",
        scaled_queries,
        gradient_heads.astype(jnp.float32),
        precision=lax.Precision.HIGHEST,
    )
    growth = jnp.exp(total)
    identity = (jnp.ones((heads,), jnp.float32), jnp.zeros((heads, width, width), jnp.float32))
    prior_memory_matrix = entering(
        (growth, running_block_state), "ctx", chain_combine, identity, False
    )[1]
    following_state = entering((growth, state_gradient), "ctx", chain_combine, identity, True)[1]
    scores = jnp.einsum("thd,shd->hts", q_heads, k_heads, preferred_element_type=jnp.float32)
    attention_result = (scores * block_weight).astype(jnp.bfloat16)
    layer_output = jnp.einsum(
        "pgm,mpo->gpo", attention_result, v_heads, preferred_element_type=jnp.float32
    )
    layer_output = layer_output + jnp.einsum(
        "bip,ipu->biu", scaled_queries, prior_memory_matrix, precision=lax.Precision.HIGHEST
    )
    dscores = jnp.einsum(
        "thd,shd->hts", gradient_heads, v_heads, preferred_element_type=jnp.float32
    )
    weight_gradient = (dscores * block_weight).astype(jnp.bfloat16)
    query_gradient = jnp.einsum(
        "pgm,mpo->gpo", weight_gradient, k_heads, preferred_element_type=jnp.float32
    )
    query_gradient = query_gradient + jnp.einsum(
        "pig,ijg->pij", scaled_gradient, prior_memory_matrix, precision=lax.Precision.HIGHEST
    )
    key_gradient = jnp.einsum(
        "nkg,knv->gnv", weight_gradient, q_heads, preferred_element_type=jnp.float32
    )
    key_gradient = key_gradient + falling_edge * jnp.einsum(
        "jnr,nbr->jnb", full_values, following_state, precision=lax.Precision.HIGHEST
    )
    value_gradient = jnp.einsum(
        "nkg,knv->gnv", attention_result, gradient_heads, preferred_element_type=jnp.float32
    )
    value_gradient = value_gradient + falling_edge * jnp.einsum(
        "umj,mje->ume", full_keys, following_state, precision=lax.Precision.HIGHEST
    )
    flat_shape = (length, queries.shape[1])
    return (
        layer_output.reshape(flat_shape).astype(jnp.bfloat16),
        query_gradient.reshape(flat_shape).astype(jnp.bfloat16),
        key_gradient.reshape(flat_shape).astype(jnp.bfloat16),
        value_gradient.reshape(flat_shape).astype(jnp.bfloat16),
    )


def route_tables(routes, route_weight, experts, capacity):
    row_count = routes.shape[0]
    flat_routes = routes.reshape(row_count * 2)
    one_hot = (flat_routes[:, None] == jnp.arange(experts, dtype=jnp.int32)[None, :]).astype(
        jnp.int32
    )
    earlier_count = jnp.cumsum(one_hot, axis=0) - one_hot
    slot_index = jnp.sum(earlier_count * one_hot, axis=1)
    target = flat_routes * capacity + slot_index
    member = (jnp.arange(experts * capacity, dtype=jnp.int32)[:, None] == target[None, :]).astype(
        jnp.float32
    )
    picker = member.reshape(experts * capacity, row_count, 2).sum(axis=2)
    merge_lookup = (
        (member * route_weight.reshape(row_count * 2)[None, :])
        .reshape(experts * capacity, row_count, 2)
        .sum(axis=2)
    )
    return (picker, merge_lookup)


def expert_terms(piece, w_gate, w_up, w_down):
    outputs = []
    for local in range(w_gate.shape[0]):
        rows = piece[:, :, local].reshape(-1, piece.shape[-1])
        gate_value = jnp.einsum(
            "md,fd->mf", rows, w_gate[local], preferred_element_type=jnp.float32
        )
        up_value = jnp.einsum("md,fd->mf", rows, w_up[local], preferred_element_type=jnp.float32)
        hidden = (jax.nn.silu(gate_value) * up_value).astype(jnp.bfloat16)
        result = jnp.dot(hidden, w_down[local], preferred_element_type=jnp.float32)
        outputs.append(
            result.reshape(piece.shape[0], piece.shape[1], piece.shape[3], piece.shape[4])
        )
    return jnp.stack(outputs, axis=2)


def experts(moe_input, routes, route_weight, w_gate, w_up, w_down):
    groups = lax.axis_size("exp")
    local_count = w_gate.shape[0]
    row_total = moe_input.shape[0]
    capacity = max(2, row_total // 2)
    picker, merge_lookup = route_tables(routes, route_weight, groups * local_count, capacity)
    departing_memory = jnp.dot(
        picker.astype(jnp.bfloat16), moe_input, preferred_element_type=jnp.float32
    ).astype(jnp.bfloat16)
    departing_memory = departing_memory.reshape(groups, local_count, capacity, moe_input.shape[1])
    arrived = lax.all_to_all(departing_memory, "exp", split_axis=0, concat_axis=0, tiled=True)
    gathered = lax.all_gather(arrived[None], "ctx", axis=0, tiled=True)
    terms = expert_terms(gathered, w_gate, w_up, w_down)
    summed = lax.psum_scatter(
        terms.astype(jnp.bfloat16), "ctx", scatter_dimension=0, tiled=True
    ).astype(jnp.float32)
    finished = summed[0].astype(jnp.bfloat16)
    returned = lax.all_to_all(finished, "exp", split_axis=0, concat_axis=0, tiled=True)
    returned = returned.reshape(groups * local_count * capacity, moe_input.shape[1])
    mixed = jnp.dot(merge_lookup.T, returned.astype(jnp.float32), precision=lax.Precision.HIGHEST)
    return mixed.astype(jnp.bfloat16)


def body(
    queries,
    attn_keys,
    attn_values,
    out_grad,
    log_decay,
    moe_input,
    routes,
    route_weight,
    w_gate,
    w_up,
    w_down,
):
    attention_parts = attention(queries, attn_keys, attn_values, out_grad, log_decay)
    moe_out = experts(moe_input, routes, route_weight, w_gate, w_up, w_down)
    return attention_parts + (moe_out,)


def solution(mesh):
    placed = (
        P("ctx", "exp"),
        P("ctx", "exp"),
        P("ctx", "exp"),
        P("ctx", "exp"),
        P("ctx", "exp"),
        P(("ctx", "exp"), None),
        P(("ctx", "exp"), None),
        P(("ctx", "exp"), None),
        P("exp", "ctx", None),
        P("exp", "ctx", None),
        P("exp", "ctx", None),
    )
    return jax.shard_map(
        body,
        mesh=mesh,
        in_specs=placed,
        out_specs=(
            P("ctx", "exp"),
            P("ctx", "exp"),
            P("ctx", "exp"),
            P("ctx", "exp"),
            P(("ctx", "exp"), None),
        ),
        check_vma=False,
    )
```

profile of v0, /device:TPU:1, one launch (start us, length us, event | category | flops | bytes accessed | tf_op | source)
XLA Modules:
  0.0 464.4 jit_solution(8278910734743402851)
XLA Ops:
  7.3 0.8 copy.166
  10.2 1.3 convolution_convert_fusion
  11.5 14.7 %all_to_all.10 = bf16[4,2,16,3072]{3,2,1,0:T(8,128)(2,1)} all-to-all(bf16[4,2,16,3072]{3,2,1,0:T(8,128)(2,1)S(1)} %bitcast.199), channel_id=1, replica_groups=mesh['ctx'=8,'exp'=4] {'exp'}, dimensions={0} | all-to-all | bytes 1572864 | tf_op jit(solution)/shard_map/all_to_all | solution.py:157
  26.9 1.1 convolution_convert_fusion.3
  28.6 1.4 convolution_convert_fusion.2
  30.8 18.1 %all-gather.3 = bf16[8,1,8]{2,1,0:T(2,128)(2,1)S(1)} all-gather(bf16[1,1,8]{2,1,0:T(2,128)(2,1)S(1)} %get-tuple-element.321), channel_id=1, replica_groups=mesh['ctx'=8,'exp'=4] {'ctx'}, dimensions={0}, use_global_device_ids=true | all-gather | bytes 144 | tf_op jit(solution)/shard_map/all_gather | solution.py:10
  49.5 75.4 %all-gather.12.cloned.1.call-done = bf16[32,2,16,3072]{3,2,1,0:T(8,128)(2,1)} async-done(((bf16[4,2,16,3072]{3,2,1,0:T(8,128)(2,1)}), bf16[32,2,16,3072]{3,2,1,0:T(8,128)(2,1)}) %all-gather.12.cloned.1.call-update) | async-done | bytes 6291472 | tf_op jit(solution)/shard_map/all_gather | solution.py:158
  125.0 3.5 fusion.74
  128.5 8.7 %fusion.8 = f32[512,1152]{1,0:T(8,128)} fusion(bf16[512,3072]{1,0:T(8,128)(2,1)S(1)} %bitcast.202, bf16[2,1152,3072]{2,1,0:T(8,128)(2,1)} %param.23), kind=kOutput, calls=%fused_computation.12 | convolution fusion | flops 3623878656 | bytes 12582912 | tf_op jit(solution)/shard_map/md,fd->mf/dot_general | solution.py:135
  137.2 5.7 %fusion.12 = f32[512,1152]{1,0:T(8,128)} fusion(bf16[512,3072]{1,0:T(8,128)(2,1)S(1)} %bitcast.200, bf16[2,1152,3072]{2,1,0:T(8,128)(2,1)S(1)} %bitcast.213), kind=kOutput, calls=%fused_computation.16 | convolution fusion | flops 3623878656 | bytes 12582912 | tf_op jit(solution)/shard_map/md,fd->mf/dot_general | solution.py:135
  142.9 8.1 %fusion.38 = bf16[512,1152]{1,0:T(8,128)(2,1)S(1)} fusion(bf16[512,3072]{1,0:T(8,128)(2,1)S(1)} %bitcast.203, bf16[2,1152,3072]{2,1,0:T(8,128)(2,1)} %param.24, f32[512,1152]{1,0:T(8,128)} %fusion.8), kind=kOutput, calls=%fused_computation.33 | convolution fusion | flops 3627417600 | bytes 13762560 | tf_op jit(solution)/shard_map/md,fd->mf/dot_general | solution.py:138
  151.1 7.3 %fusion.41 = bf16[512,1152]{1,0:T(8,128)(2,1)S(1)} fusion(bf16[512,3072]{1,0:T(8,128)(2,1)S(1)} %bitcast.201, bf16[2,1152,3072]{2,1,0:T(8,128)(2,1)} %param.24, f32[512,1152]{1,0:T(8,128)S(1)} %copy-done.8), kind=kOutput, calls=%fused_computation.34 | convolution fusion | flops 3627417600 | bytes 13762560 | tf_op jit(solution)/shard_map/md,fd->mf/dot_general | solution.py:138
  158.4 7.6 %fusion.26 = bf16[8,4,1,16,3072]{4,3,1,0,2:T(8,128)(2,1)S(1)} fusion(bf16[8,4,16,1152]{3,2,1,0:T(8,128)(2,1)S(1)} %bitcast.214, bf16[2,1152,3072]{2,1,0:T(8,128)(2,1)} %param.25), kind=kOutput, calls=%fused_computation.27 | convolution fusion | flops 3625451520 | bytes 11403264 | tf_op jit(solution)/shard_map/dot_general | solution.py:140
  166.0 7.7 %fusion.29 = bf16[8,4,1,16,3072]{4,3,1,0,2:T(8,128)(2,1)S(1)} fusion(bf16[8,4,16,1152]{3,2,1,0:T(8,128)(2,1)S(1)} %bitcast.215, bf16[2,1152,3072]{2,1,0:T(8,128)(2,1)} %param.25), kind=kOutput, calls=%fused_computation.28 | convolution fusion | flops 3625451520 | bytes 11403264 | tf_op jit(solution)/shard_map/dot_general | solution.py:140
  173.8 3.2 pad_maximum_fusion
  177.0 9.1 %while.30 = (s32[]{:T(128)}, f32[8,128,128]{2,1,0:T(8,128)S(1)}, s32[]{:T(128)}, bf16[8,8]{1,0:T(8,128)(2,1)S(1)}, bf16[8,8,128,128]{3,2,1,0:T(8,128)(2,1)}, /*index=5*/s32[]{:T(128)}, s32[]{:T(128)}) while((s32[]{:T(128)}, f32[8,128,128]{2,1,0:T(8,128)S(1)}, s32[]{:T(128)}, bf16[8,8]{1,0:T(8,128)(2,1)S(1)}, ...), condition=%wide.region_2.3_spmd.clone, body=%wide.region_1.2_spmd.clone.sunk | while | flops 655372 | bytes 1310913 | solution.py:28
  177.0 1.1 fusion.108
  178.2 1.1 fusion.108
  179.3 1.1 fusion.108
  180.4 1.1 fusion.108
  181.6 1.1 fusion.108
  182.7 1.1 fusion.108
  183.8 1.1 fusion.108
  185.0 1.1 fusion.108
  186.8 1.0 fusion.54
  187.8 37.0 %all-gather.10.cloned.1.call-done = bf16[64,128,128]{2,1,0:T(8,128)(2,1)} async-done(((bf16[8,128,128]{2,1,0:T(8,128)(2,1)}), bf16[64,128,128]{2,1,0:T(8,128)(2,1)}) %all-gather.10.cloned.1.call-update) | async-done | bytes 2097168 | tf_op jit(solution)/shard_map/all_gather | solution.py:10
  224.8 9.1 %while.31 = (s32[]{:T(128)}, f32[8,128,128]{2,1,0:T(8,128)S(1)}, s32[]{:T(128)}, bf16[8,8]{1,0:T(8,128)(2,1)S(1)}, bf16[8,8,128,128]{3,2,1,0:T(8,128)(2,1)}, /*index=5*/s32[]{:T(128)}, s32[]{:T(128)}, s32[]{:T(128)}, s32[]{:T(128)}) while((s32[]{:T(128)}, f32[8,128,128]{2,1,0:T(8,128)S(1)}, s32[]{:T(128)}, ...), condition=%wide.region_4.5_spmd.clone, body=%wide.region_3.4_spmd.clone.sunk | while | flops 655376 | bytes 1310975 | solution.py:28
  224.8 1.1 fusion.109
  225.9 1.1 fusion.109
  227.0 1.1 fusion.109
  228.2 1.1 fusion.109
  229.3 1.1 fusion.109
  230.5 1.1 fusion.109
  231.6 1.1 fusion.109
  232.8 1.1 fusion.109
  234.5 0.9 fusion.53
  235.5 1.0 convolution_bitcast_fusion.7
  236.5 202.3 %all-reduce.3.cloned.1.call-done = bf16[8,4,2,16,3072]{4,3,1,0,2:T(8,128)(2,1)} async-done(((bf16[8,4,2,16,3072]{4,3,1,0,2:T(8,128)(2,1)}), bf16[8,4,2,16,3072]{4,3,1,0,2:T(8,128)(2,1)}) %all-reduce.3.cloned.1.call-update) | async-done | bytes 6291472
  438.8 1.8 dynamic-slice_bitcast_fusion
  440.7 1.0 copy.168
  441.6 4.5 all-to-all-start.1
  446.1 1.0 fusion.55
  447.1 1.8 copy.169
  448.9 0.8 copy.170
  449.8 0.8 copy.171
  451.4 0.8 copy.172
  452.3 4.5 all-to-all-done.1
  456.7 1.1 convolution_convert_fusion.1
  (81 shorter events, 6.9 us)
Async XLA Ops:
  7.2 19.8 %copy-start = (bf16[128,1024]{1,0:T(8,128)(2,1)S(1)}, bf16[128,1024]{1,0:T(8,128)(2,1)}, u32[]{:S(2)}) copy-start(bf16[128,1024]{1,0:T(8,128)(2,1)} %param.17) | copy-start | bytes 786436
  7.2 19.2 %copy-start.6 = (f32[128,8]{0,1:T(8,128)S(1)}, f32[128,8]{0,1:T(8,128)}, u32[]{:S(2)}) copy-start(f32[128,8]{0,1:T(8,128)} %param.19) | copy-start | bytes 12292
  7.2 19.3 %copy-start.3 = (bf16[128,1024]{1,0:T(8,128)(2,1)S(1)}, bf16[128,1024]{1,0:T(8,128)(2,1)}, u32[]{:S(2)}) copy-start(bf16[128,1024]{1,0:T(8,128)(2,1)} %param.16) | copy-start | bytes 786436
  7.2 20.9 %copy-start.4 = (bf16[128,1024]{1,0:T(8,128)(2,1)S(1)}, bf16[128,1024]{1,0:T(8,128)(2,1)}, u32[]{:S(2)}) copy-start(bf16[128,1024]{1,0:T(8,128)(2,1)} %param.15) | copy-start | bytes 786436
  7.2 21.2 %copy-start.5 = (bf16[128,1024]{1,0:T(8,128)(2,1)S(1)}, bf16[128,1024]{1,0:T(8,128)(2,1)}, u32[]{:S(2)}) copy-start(bf16[128,1024]{1,0:T(8,128)(2,1)} %param.18) | copy-start | bytes 786436
  7.2 117.8 %all-gather.12.cloned.1.call-start = ((), (), s32[]{:S(2)}) async-start(), calls=%async_computation.4 | async-start | bytes 7077888 | tf_op jit(solution)/shard_map/all_gather | solution.py:158
  26.3 150.7 %all-gather.8.cloned.1.call-start = ((), (), s32[]{:S(2)}) async-start(), calls=%async_computation.2 | async-start | bytes 2359296 | tf_op jit(solution)/shard_map/all_gather | solution.py:10
  26.9 22.1 %copy-start.7 = (u32[32]{0:T(128)S(1)}, u32[32]{0:T(128)}, u32[]{:S(2)}) copy-start(u32[32]{0:T(128)} %constant.94) | copy-start | bytes 388
  28.1 196.7 %all-gather.10.cloned.1.call-start = ((), (), s32[]{:S(2)}) async-start(), calls=%async_computation.3 | async-start | bytes 2359296 | tf_op jit(solution)/shard_map/all_gather | solution.py:10
  30.0 408.9 %all-reduce.3.cloned.1.call-start = ((), (), s32[]{:S(2)}) async-start(), calls=%async_computation.5 | async-start | bytes 12582912
  125.0 12.2 %slice-start = ((s8[14155776]{0:T(1024)(128)(4,1)}), s8[4194304]{0:T(1024)(128)(4,1)S(1)}, s32[]{:S(2)}) async-start(s8[14155776]{0:T(1024)(128)(4,1)} %bitcast.212), calls=%async_computation.6 | async-start | bytes 8388608
  125.0 12.2 %slice-start.1 = ((s8[14155776]{0:T(1024)(128)(4,1)}), s8[4194304]{0:T(1024)(128)(4,1)S(1)}, s32[]{:S(2)}) async-start(s8[14155776]{0:T(1024)(128)(4,1)} %bitcast.212), calls=%async_computation.7 | async-start | bytes 8388608
  128.5 8.7 %slice-start.2 = ((s8[14155776]{0:T(1024)(128)(4,1)}), s8[4194304]{0:T(1024)(128)(4,1)S(1)}, s32[]{:S(2)}) async-start(s8[14155776]{0:T(1024)(128)(4,1)} %bitcast.212), calls=%async_computation.8 | async-start | bytes 8388608
  128.5 8.7 %slice-start.3 = ((s8[14155776]{0:T(1024)(128)(4,1)}), s8[1572864]{0:T(1024)(128)(4,1)S(1)}, s32[]{:S(2)}) async-start(s8[14155776]{0:T(1024)(128)(4,1)} %bitcast.212), calls=%async_computation.9 | async-start | bytes 3145728
  142.9 8.1 %copy-start.8 = (f32[512,1152]{1,0:T(8,128)S(1)}, f32[512,1152]{1,0:T(8,128)}, u32[]{:S(2)}) copy-start(f32[512,1152]{1,0:T(8,128)} %fusion.12) | copy-start | bytes 7077892
  438.8 10.1 %copy-start.1 = (bf16[128,8,128]{0,2,1:T(8,128)(2,1)S(1)}, bf16[128,8,128]{0,2,1:T(8,128)(2,1)}, u32[]{:S(2)}) copy-start(bf16[128,8,128]{0,2,1:T(8,128)(2,1)} %fusion.54) | copy-start | bytes 786436
  440.6 9.1 %copy-start.2 = (bf16[128,8,128]{0,2,1:T(8,128)(2,1)S(1)}, bf16[128,8,128]{0,2,1:T(8,128)(2,1)}, u32[]{:S(2)}) copy-start(bf16[128,8,128]{0,2,1:T(8,128)(2,1)} %fusion.53) | copy-start | bytes 786436
  441.6 15.1 %all-to-all-start.1 = ((bf16[4,2,16,3072]{3,2,1,0:T(8,128)(2,1)}), bf16[4,2,16,3072]{3,2,1,0:T(8,128)(2,1)S(1)}, u32[]{:S(2)}, u32[]{:S(2)}) async-start(bf16[4,2,16,3072]{3,2,1,0:T(8,128)(2,1)} %copy.168), calls=%async_computation.1 | async-start | bytes 1572864 | tf_op jit(solution)/shard_map/all_to_all | solution.py:164
Sparse Core Ops, SparseCore 0:
  26.4 98.5 all-gather.11
  127.7 46.6 all-gather.7
  177.1 47.5 all-gather.9
  228.4 210.4 all-reduce.2
where the time goes:
time: 466 us; the launch traced here: 464 us
  waiting for transfers between devices  319 us (68%)
  matrix products  56.9 us (12%)
  blocking collectives  32.9 us (7%)
  other arithmetic  22.8 us (5%)
  between operations  14.1 us (3%)
  local copies, waits for them, and re-layouts  13.2 us (3%)
    unnamed x5, waiting for transfers between devices  202 us
    all_gather x1, waiting for transfers between devices, experts(): gathered = lax.all_gather(arrived[None], 'ctx', axis=0, tiled=True)  75.4 us
    all_gather x2, waiting for transfers between devices, entering(): lax.all_gather(part.astype(kind), axis)  37 us
    all_gather x1, blocking collectives, entering(): lax.all_gather(part.astype(kind), axis)  18.1 us
    select_n x16, other arithmetic, step(): return jax.tree.map(lambda a, b: jnp.where(reached, a, b), new, before)  17.5 us
    dot_general x2, matrix products, expert_terms(): jnp.einsum('md,fd->mf', rows, w_up[local], preferred_element_type=jnp.flo...  15.4 us
    dot_general x2, matrix products, expert_terms(): result = jnp.dot(hidden, w_down[local], preferred_element_type=jnp.float32)  15.4 us
    all_to_all x1, blocking collectives, experts(): lax.all_to_all(departing_memory, 'exp', split_axis=0, concat_axis=0, tile...  14.7 us
  transfers between devices with their start and end apart: 5, of which 4 were waited for; matrix products, arithmetic and copies ran while one was open for 18% of the time, Pallas kernels for 0%

commit v1 on v0

v1 whole, which is shorter than its diff:
```python
import jax
import jax.numpy as jnp
from jax import lax
from jax.experimental import pallas as pl
from jax.experimental.pallas import tpu as pltpu
from jax.sharding import PartitionSpec as P

BF = jnp.bfloat16
F32 = jnp.float32
BOTH = ("ctx", "exp")
SIDE = 128


def dg(a, b, ca, cb):
    return lax.dot_general(a, b, (((ca,), (cb,)), ((), ())), preferred_element_type=F32)


def block_of(total, top):
    if total <= top:
        return total
    for b in range(top, 0, -128):
        if total % b == 0:
            return b
    return total


class Plan:
    def __init__(self, n_ctx, n_exp):
        self.n_ctx, self.n_exp = n_ctx, n_exp
        self.cores = 2 if n_exp % 2 == 0 else 1
        nx = n_exp // self.cores
        ny = 1 << (max(0, n_ctx.bit_length() - 1) // 2)
        nz = n_ctx // ny
        bits = lambda axis, n: [(axis, 1 << k) for k in range(n.bit_length() - 1)]
        zs, ys, xs = bits("z", nz)[::-1], bits("y", ny), bits("x", nx)
        self.ny = ny
        self.orders = (zs + xs + ys, ys + zs + xs)
        if not xs:
            self.orders = (zs + ys, zs + ys)
        self.stages = len(self.orders[0])

    def place(self, i):
        c, e = divmod(i, self.n_exp)
        z, y = divmod(c, self.ny)
        x, core = divmod(e, self.cores)
        return {"z": z, "y": y, "x": x, "core": core}

    def index(self, p):
        return (p["z"] * self.ny + p["y"]) * self.n_exp + p["x"] * self.cores + p["core"]

    def flip(self, pick):
        out = []
        for i in range(self.n_ctx * self.n_exp):
            p = self.place(i)
            axis, bit = pick(p)
            p[axis] ^= bit
            out.append((i, self.index(p)))
        return out

    def stage(self, k):
        return self.flip(lambda p: self.orders[p["core"]][k])

    def mate(self):
        return self.flip(lambda p: ("core", 1))

    def block(self, bit):
        return [(i, (c ^ bit) * self.n_exp + e) for i in range(self.n_ctx * self.n_exp) for c, e in [divmod(i, self.n_exp)]]


def send(value, pairs):
    return lax.ppermute(value, BOTH, pairs)


def decays(ld_ref, g_ref):
    n = ld_ref.shape[0]
    low = (lax.broadcasted_iota(jnp.int32, (n, n), 0) >= lax.broadcasted_iota(jnp.int32, (n, n), 1)).astype(F32)
    g_ref[...] = lax.dot_general(
        low, ld_ref[...], (((1,), (0,)), ((), ())), precision=lax.Precision.HIGHEST, preferred_element_type=F32
    )


def column(g_ref, h):
    g = g_ref[...]
    lane = lax.broadcasted_iota(jnp.int32, g.shape, 1)
    return jnp.sum(jnp.where(lane == h, g, 0.0), axis=1, keepdims=True)


def states(q, k, v, d, ld):
    n, heads = ld.shape
    w = q.shape[1] // heads

    def kern(q_r, k_r, v_r, d_r, ld_r, b_r, c_r, g_r):
        h = pl.program_id(0)

        @pl.when(h == 0)
        def _():
            decays(ld_r, g_r)

        g = column(g_r, h)
        fall = jnp.exp(g[n - 1 : n, :] - g)
        b_r[0] = dg((k_r[...].astype(F32) * fall).astype(BF), v_r[...], 0, 0).astype(BF)
        c_r[0] = dg((q_r[...].astype(F32) * jnp.exp(g)).astype(BF), d_r[...], 0, 0).astype(BF)

    tile = pl.BlockSpec((n, w), lambda h: (0, h))
    whole = pl.BlockSpec((n, heads), lambda h: (0, 0))
    out = pl.BlockSpec((1, w, w), lambda h: (h, 0, 0))
    return pl.pallas_call(
        kern,
        grid=(heads,),
        in_specs=[tile] * 4 + [whole],
        out_specs=[out, out],
        out_shape=[jax.ShapeDtypeStruct((heads, w, w), BF)] * 2,
        scratch_shapes=[pltpu.VMEM((n, heads), F32)],
        compiler_params=pltpu.CompilerParams(dimension_semantics=("arbitrary",)),
    )(q, k, v, d, ld)


def finish(q, k, v, d, ld, s, r):
    n, heads = ld.shape
    w = q.shape[1] // heads

    def kern(q_r, k_r, v_r, d_r, ld_r, s_r, r_r, o_r, gq_r, gk_r, gv_r, g_r):
        h = pl.program_id(0)

        @pl.when(h == 0)
        def _():
            decays(ld_r, g_r)

        g = column(g_r, h)
        rise = jnp.exp(g)
        fall = jnp.exp(g[n - 1 : n, :] - g)
        wide = jnp.broadcast_to(g, (n, n))
        causal = lax.broadcasted_iota(jnp.int32, (n, n), 0) >= lax.broadcasted_iota(jnp.int32, (n, n), 1)
        weight = jnp.where(causal, jnp.exp(jnp.where(causal, wide - wide.T, 0.0)), 0.0)
        qh, kh, vh, dh = q_r[...], k_r[...], v_r[...], d_r[...]
        sh, rh = s_r[0].astype(BF), r_r[0].astype(BF)
        attn = (dg(qh, kh, 1, 1) * weight).astype(BF)
        grad = (dg(dh, vh, 1, 1) * weight).astype(BF)
        o_r[...] = (dg(attn, vh, 1, 0) + rise * dg(qh, sh, 1, 0)).astype(BF)
        gq_r[...] = (dg(grad, kh, 1, 0) + rise * dg(dh, sh, 1, 1)).astype(BF)
        gk_r[...] = (dg(grad, qh, 0, 0) + fall * dg(vh, rh, 1, 1)).astype(BF)
        gv_r[...] = (dg(attn, dh, 0, 0) + fall * dg(kh, rh, 1, 0)).astype(BF)

    tile = pl.BlockSpec((n, w), lambda h: (0, h))
    whole = pl.BlockSpec((n, heads), lambda h: (0, 0))
    state = pl.BlockSpec((1, w, w), lambda h: (h, 0, 0))
    return pl.pallas_call(
        kern,
        grid=(heads,),
        in_specs=[tile] * 4 + [whole, state, state],
        out_specs=[tile] * 4,
        out_shape=[jax.ShapeDtypeStruct(q.shape, BF)] * 4,
        scratch_shapes=[pltpu.VMEM((n, heads), F32)],
        compiler_params=pltpu.CompilerParams(dimension_semantics=("arbitrary",)),
    )(q, k, v, d, ld, s, r)


def parts(x, count):
    out = []
    for _ in range(count):
        p = lax.reduce_precision(x, 8, 7)
        out.append(p.astype(BF))
        x = x - p
    return out


def scan_states(b, c, growth, plan):
    heads, w, _ = b.shape
    here = lax.axis_index("ctx")
    s = r = jnp.zeros((heads, w, w), F32)
    before = after = jnp.ones((heads,), F32)
    total = growth
    wide = lambda a: a[:, None, None]
    bit = 1
    while bit < plan.n_ctx:
        extra = jnp.stack(parts(total, 3)).reshape(1, 3 * heads)
        extra = jnp.pad(extra, ((0, w - 1), (0, w - 3 * heads)))[None]
        got = send(jnp.concatenate([b.astype(BF), c.astype(BF), extra]), plan.block(bit))
        b2, c2 = got[:heads].astype(F32), got[heads : 2 * heads].astype(F32)
        t2 = got[2 * heads, 0, : 3 * heads].astype(F32).reshape(3, heads).sum(axis=0)
        b1, c1 = b.astype(F32), c.astype(F32)
        upper = (here & bit) != 0
        s = jnp.where(upper, s + wide(before) * b2, s)
        r = jnp.where(upper, r, r + wide(after) * c2)
        before = jnp.where(upper, before * t2, before)
        after = jnp.where(upper, after, after * t2)
        b = jnp.where(upper, wide(total) * b2 + b1, wide(t2) * b1 + b2)
        c = jnp.where(upper, c2 + wide(t2) * c1, c1 + wide(total) * c2)
        total = total * t2
        bit *= 2
    return s, r


def expert_half(tokens, first, w_gate, w_up, w_down):
    n = len(tokens)
    rows, wide = tokens[0].shape
    count, hidden, width = w_gate.shape
    fb, db = block_of(hidden, 384), block_of(width, 1024)
    nf, nd = hidden // fb, width // db
    blk = rows
    while blk > 256 and blk % 2 == 0:
        blk //= 2
    cap = blk // 2
    per = rows // blk
    places = [(i, j, i * per + j) for i in range(n) for j in range(per)]
    up_steps = count * nf

    def kern(first_r, *refs):
        tin = refs[:n]
        wg_r, wu_r, wd_r = refs[n : n + 3]
        outs = refs[n + 3 : 2 * n + 3]
        xs, hid, wcol, pt = refs[2 * n + 3 :]
        t = pl.program_id(0)

        def gather(e):
            eid = (first_r[0] + e).astype(F32)
            tri = lax.broadcasted_iota(jnp.int32, (blk, blk), 0) > lax.broadcasted_iota(jnp.int32, (blk, blk), 1)
            slot = lax.broadcasted_iota(jnp.int32, (blk, cap), 1).astype(F32)
            for i, j, b in places:
                side = tin[i][pl.ds(j * blk, blk), width : width + SIDE].astype(F32)
                named = (side[:, 0:1] == eid) | (side[:, 1:2] == eid)
                named = jnp.broadcast_to(named.astype(F32), (blk, cap))
                rank = dg(tri.astype(BF), named.astype(BF), 1, 0)
                member = jnp.where((rank == slot) & (named > 0.0), 1.0, 0.0)
                pt[e, pl.ds(b * blk, blk), :] = member.astype(BF)
                pick = member.T.astype(BF)
                xs[pl.ds(b * cap, cap), :] = dg(pick, tin[i][pl.ds(j * blk, blk), 0:width], 1, 0).astype(BF)
                got = dg(pick, side.astype(BF), 1, 0)
                w0 = got[:, 2:3] + got[:, 3:4] + got[:, 4:5]
                w1 = got[:, 5:6] + got[:, 6:7] + got[:, 7:8]
                scale = jnp.where(got[:, 0:1] == eid, w0, w1)
                wcol[e, pl.ds(b * cap, cap), :] = jnp.broadcast_to(scale, (cap, SIDE))

        for e in range(count):
            for f in range(nf):

                @pl.when(t == e * nf + f)
                def _(e=e, f=f):
                    if f == 0:
                        gather(e)
                    x = xs[...]
                    gate = dg(wg_r[0], x, 1, 1)
                    up = dg(wu_r[0], x, 1, 1)
                    act = gate / (1.0 + jnp.exp(-gate)) * up
                    hid[e, :, f * fb : (f + 1) * fb] = act.T.astype(BF)

        @pl.when(t >= up_steps)
        def _():
            res = [(dg(hid[e], wd_r[e], 1, 0) * wcol[e, :, 0:1]).astype(BF) for e in range(count)]
            for i, j, b in places:
                mix = sum(dg(pt[e, pl.ds(b * blk, blk), :], res[e][b * cap : (b + 1) * cap], 1, 0) for e in range(count))
                outs[i][pl.ds(j * blk, blk), :] = mix.astype(BF)

    def up_map(t, s):
        q = jnp.minimum(t, up_steps - 1)
        return (q // nf, q % nf, 0)

    def down_map(t, s):
        return (0, 0, jnp.maximum(t - up_steps, 0))

    def out_map(t, s):
        return (0, jnp.maximum(t - up_steps, 0))

    held = pl.BlockSpec((rows, wide), lambda t, s: (0, 0), pipeline_mode=pl.Buffered(1))
    slots = len(places) * cap
    return pl.pallas_call(
        kern,
        out_shape=[jax.ShapeDtypeStruct((rows, width), BF)] * n,
        grid_spec=pltpu.PrefetchScalarGridSpec(
            num_scalar_prefetch=1,
            grid=(up_steps + nd,),
            in_specs=[held] * n + [pl.BlockSpec((1, fb, width), up_map)] * 2 + [pl.BlockSpec((count, hidden, db), down_map)],
            out_specs=[pl.BlockSpec((rows, db), out_map)] * n,
            scratch_shapes=[
                pltpu.VMEM((slots, width), BF),
                pltpu.VMEM((count, slots, hidden), BF),
                pltpu.VMEM((count, slots, SIDE), F32),
                pltpu.VMEM((count, len(places) * blk, cap), BF),
            ],
        ),
        compiler_params=pltpu.CompilerParams(dimension_semantics=("arbitrary",), vmem_limit_bytes=58 * 2**20),
    )(first, *tokens, w_gate, w_up, w_down)


def add(a, b):
    return (a.astype(F32) + b.astype(F32)).astype(BF)


def halve(own, other, plan):
    parts_ = (own, other)
    for k in range(plan.stages - 2, -1, -1):
        half = parts_[0].shape[0] // 2
        away = add(parts_[0][half:], parts_[1][half:])
        stay = add(parts_[0][:half], parts_[1][:half])
        parts_ = (stay, send(away, plan.stage(k)))
    return add(*parts_)


def body(queries, attn_keys, attn_values, out_grad, log_decay, moe_input, routes, route_weight, w_gate, w_up, w_down):
    plan = Plan(lax.axis_size("ctx"), lax.axis_size("exp"))
    rows, width = moe_input.shape
    first = (lax.axis_index("exp") * w_gate.shape[0]).astype(jnp.int32).reshape(1)

    cols = [routes[:, 0].astype(BF), routes[:, 1].astype(BF)]
    cols += parts(route_weight[:, 0], 3) + parts(route_weight[:, 1], 3)
    side = jnp.pad(jnp.stack(cols, axis=1), ((0, 0), (0, SIDE - len(cols))))
    near = jnp.concatenate([moe_input, side], axis=1)
    for k in range(plan.stages - 1):
        near = jnp.concatenate([near, send(near, plan.stage(k))], axis=0)
    last = plan.stage(plan.stages - 1)
    far = send(near, last)
    near_mate = send(near, plan.mate())

    b, c = states(queries, attn_keys, attn_values, out_grad, log_decay)
    growth = jnp.exp(jnp.sum(log_decay, axis=0))
    s, r = scan_states(b, c, growth, plan)

    near_own, near_other = expert_half([near, near_mate], first, w_gate, w_up, w_down)
    far_mate = send(far, plan.mate())
    near_back = send(near_other, plan.mate())
    far_own, far_other = expert_half([far, far_mate], first, w_gate, w_up, w_down)
    far_back = send(far_other, plan.mate())
    near_sum = halve(near_own, near_back, plan)
    far_sum = halve(far_own, far_back, plan)
    moe_out = add(near_sum, send(far_sum, last))
    results = finish(queries, attn_keys, attn_values, out_grad, log_decay, s, r)
    return tuple(results) + (moe_out,)


def solution(mesh):
    token = P("ctx", "exp")
    row = P(BOTH, None)
    weight = P("exp", "ctx", None)
    return jax.shard_map(
        body,
        mesh=mesh,
        in_specs=(token,) * 5 + (row,) * 3 + (weight,) * 3,
        out_specs=(token,) * 4 + (row,),
        check_vma=False,
    )
```

time: 466 us -> 213 us (0.46)
  waiting for transfers between devices: 319 us -> 76.8 us
  Pallas kernels: 0 us -> 67.2 us
  matrix products: 56.9 us -> 0 us
  starting transfers between devices: 4.64 us -> 49.7 us
  blocking collectives: 32.9 us -> 0 us
  between operations: 14.1 us -> 0.83 us
  local copies, waits for them, and re-layouts: 13.2 us -> 1.51 us
  other arithmetic: 22.8 us -> 15.6 us
    unnamed x5 -> x0, waiting for transfers between devices: 202 us -> none
    all_gather x3 -> x0, waiting for transfers between devices: 112 us -> none  [the longest x1 75.4 us: experts(): gathered = lax.all_gather(arrived[None], 'ctx', axis=0, tiled=True)]
    ppermute x0 -> x18, waiting for transfers between devices: none -> 76.8 us  [send(): return lax.ppermute(value, BOTH, pairs)]
    pallas_call x0 -> x4, Pallas kernels: none -> 67.2 us  [the longest x2 54 us: expert_half(): pl.pallas_call(kern, out_shape=[jax.ShapeDtypeStruct((rows, width), BF)]...]
    dot_general x20 -> x0, matrix products: 56.9 us -> none  [the longest x2 15.4 us: expert_terms(): jnp.einsum('md,fd->mf', rows, w_up[local], preferred_element_type=jnp.flo...]
    ppermute x0 -> x18, starting transfers between devices: none -> 49.7 us  [send(): return lax.ppermute(value, BOTH, pairs)]
    all_gather x1 -> x0, blocking collectives: 18.1 us -> none  [entering(): lax.all_gather(part.astype(kind), axis)]
    select_n x16 -> x2, other arithmetic: 17.5 us -> 1.46 us  [the longest x1 1.45 us: scan_states(): r = jnp.where(upper, r, r + wide(after) * c2)]
  transfers between devices with their start and end apart: 5 -> 18, of which waited for: 4 -> 7; matrix products, arithmetic and copies ran while one was open for 18% -> 5% of each run, Pallas kernels for 0% -> 32%
where the time goes in v1:
time: 213 us; the launch traced here: 212 us
  waiting for transfers between devices  76.8 us (36%)
  Pallas kernels  67.2 us (32%)
  starting transfers between devices  49.7 us (23%)
  other arithmetic  15.6 us (7%)
    ppermute x18, waiting for transfers between devices, send(): return lax.ppermute(value, BOTH, pairs)  76.8 us
    pallas_call x2, Pallas kernels, expert_half(): pl.pallas_call(kern, out_shape=[jax.ShapeDtypeStruct((rows, width), BF)]...  54 us
    ppermute x18, starting transfers between devices, send(): return lax.ppermute(value, BOTH, pairs)  49.7 us
    pallas_call x1, Pallas kernels, finish(): pl.pallas_call(kern, grid=(heads,), in_specs=[tile] * 4 + [whole, state,...  7.06 us
    pallas_call x1, Pallas kernels, states(): pl.pallas_call(kern, grid=(heads,), in_specs=[tile] * 4 + [whole], out_sp...  6.12 us
    convert_element_type x8, other arithmetic, add(): return (a.astype(F32) + b.astype(F32)).astype(BF)  5.33 us
  transfers between devices with their start and end apart: 18, of which 7 were waited for; matrix products, arithmetic and copies ran while one was open for 5% of the time, Pallas kernels for 32%

profile of v1, /device:TPU:1, one launch (start us, length us, event | category | flops | bytes accessed | tf_op | source)
XLA Modules:
  0.0 211.7 jit_solution(10440046653716233941)
XLA Ops:
  0.6 0.8 fusion.19
  1.4 0.7 convert.6
  2.1 0.1 copy.25
  2.2 0.9 pad_maximum_fusion.6
  3.2 2.1 %collective-permute-start.3 = (bf16[32,3200]{1,0:T(8,128)(2,1)S(1)}, bf16[32,3200]{1,0:T(8,128)(2,1)S(1)}, u32[]{:S(2)}, u32[]{:S(2)}) collective-permute-start(bf16[32,3200]{1,0:T(8,128)(2,1)S(1)} %pad_maximum_fusion.6), channel_id=1, source_target_pairs={{0,16},{1,5},{2,18},{3,7},{4,20},{5,1},{6,22},{7,3},{8,24},{9,13},... | collective-permute-start | bytes 614408 | tf_op jit(solution)/shard_map/ppermute | solution.py:71
  5.3 3.4 %collective-permute-done.3 = bf16[32,3200]{1,0:T(8,128)(2,1)S(1)} collective-permute-done((bf16[32,3200]{1,0:T(8,128)(2,1)S(1)}, bf16[32,3200]{1,0:T(8,128)(2,1)S(1)}, u32[]{:S(2)}, u32[]{:S(2)}) %collective-permute-start.3) | collective-permute-done | bytes 204832 | tf_op jit(solution)/shard_map/ppermute | solution.py:71
  8.7 1.0 pad_maximum_fusion.5
  9.7 2.6 %collective-permute-start.4 = (bf16[64,3200]{1,0:T(8,128)(2,1)S(1)}, bf16[64,3200]{1,0:T(8,128)(2,1)S(1)}, u32[]{:S(2)}, u32[]{:S(2)}) collective-permute-start(bf16[64,3200]{1,0:T(8,128)(2,1)S(1)} %pad_maximum_fusion.5), channel_id=1, source_target_pairs={{0,8},{1,17},{2,10},{3,19},{4,12},{5,21},{6,14},{7,23},{8,0},{9,25... | collective-permute-start | bytes 1228808 | tf_op jit(solution)/shard_map/ppermute | solution.py:71
  12.3 9.8 %collective-permute-done.4 = bf16[64,3200]{1,0:T(8,128)(2,1)S(1)} collective-permute-done((bf16[64,3200]{1,0:T(8,128)(2,1)S(1)}, bf16[64,3200]{1,0:T(8,128)(2,1)S(1)}, u32[]{:S(2)}, u32[]{:S(2)}) %collective-permute-start.4) | collective-permute-done | bytes 409632 | tf_op jit(solution)/shard_map/ppermute | solution.py:71
  22.1 1.0 pad_maximum_fusion.1
  23.2 0.7 collective-permute-start.5
  23.9 10.8 %collective-permute-done.5 = bf16[128,3200]{1,0:T(8,128)(2,1)S(1)} collective-permute-done((bf16[128,3200]{1,0:T(8,128)(2,1)S(1)}, bf16[128,3200]{1,0:T(8,128)(2,1)S(1)}, u32[]{:S(2)}, u32[]{:S(2)}) %collective-permute-start.5) | collective-permute-done | bytes 819232 | tf_op jit(solution)/shard_map/ppermute | solution.py:71
  34.7 0.1 pad_maximum_fusion.refs_0_
  34.9 1.3 collective-permute-start.11
  36.2 0.7 copy.24.ld_r
  36.9 0.1 reduce_sum.31
  37.1 6.1 %shard_map.146 = (bf16[8,128,128]{2,1,0:T(8,128)(2,1)}, bf16[8,128,128]{2,1,0:T(8,128)(2,1)}) custom-call(bf16[128,1024]{1,0:T(8,128)(2,1)} %q_r.3, bf16[128,1024]{1,0:T(8,128)(2,1)} %k_r.3, bf16[128,1024]{1,0:T(8,128)(2,1)} %v_r.3, bf16[128,1024]{1,0:T(8,128)(2,1)} %d_r.3, f32[128,8]{1,0:T(8,128)} %copy.24.ld_r), custom_call_target="tpu_custom_call" | custom-call | tf_op jit(solution)/shard_map/pallas_call | solution.py:107
  43.3 1.1 pad_maximum_fusion.2
  44.4 1.3 collective-permute-start
  45.7 10.5 %collective-permute-done.11.refs_0_ = bf16[256,3200]{1,0:T(8,128)(2,1)} collective-permute-done((bf16[256,3200]{1,0:T(8,128)(2,1)S(1)}, bf16[256,3200]{1,0:T(8,128)(2,1)}, u32[]{:S(2)}, u32[]{:S(2)}) %collective-permute-start.11) | collective-permute-done | bytes 1638432 | tf_op jit(solution)/shard_map/ppermute | solution.py:71
  56.2 11.2 %collective-permute-start.12 = (bf16[256,3200]{1,0:T(8,128)(2,1)}, bf16[256,3200]{1,0:T(8,128)(2,1)}, u32[]{:S(2)}, u32[]{:S(2)}) collective-permute-start(bf16[256,3200]{1,0:T(8,128)(2,1)} %collective-permute-done.11.refs_0_), channel_id=1, source_target_pairs={{0,1},{1,0},{2,3},{3,2},{4,5},{5,4},{6,7},{7,6},{8,9},{9,8},{10,11... | collective-permute-start | bytes 4915208 | tf_op jit(solution)/shard_map/ppermute | solution.py:71
  67.5 5.9 %collective-permute-start.6 = (bf16[256,3200]{1,0:T(8,128)(2,1)S(1)}, bf16[256,3200]{1,0:T(8,128)(2,1)}, u32[]{:S(2)}, u32[]{:S(2)}) collective-permute-start(bf16[256,3200]{1,0:T(8,128)(2,1)S(1)} %pad_maximum_fusion.refs_0_), channel_id=1, source_target_pairs={{0,1},{1,0},{2,3},{3,2},{4,5},{5,4},{6,7},{7,6},{8,9},{9,8},{10,11... | collective-permute-start | bytes 4915208 | tf_op jit(solution)/shard_map/ppermute | solution.py:71
  73.5 1.4 fusion.9
  75.0 0.9 pad_maximum_fusion.3
  75.8 26.9 %shard_map.149 = (bf16[256,3072]{1,0:T(8,128)(2,1)}, bf16[256,3072]{1,0:T(8,128)(2,1)}) custom-call(s32[1]{0:T(128)} %bitcast.6.first_r, bf16[256,3200]{1,0:T(8,128)(2,1)} %collective-permute-done.11.refs_0_, bf16[256,3200]{1,0:T(8,128)(2,1)} %collective-permute-done.12.refs_1_, bf16[2,1152,3072]{2,1,0:T(8,128)(2,1)} %refs_2_.3, ...), custom_call_target="tpu_custom_call" | custom-call | tf_op jit(solution)/shard_map/pallas_call | solution.py:266
  102.9 27.1 %shard_map.148 = (bf16[256,3072]{1,0:T(8,128)(2,1)}, bf16[256,3072]{1,0:T(8,128)(2,1)}) custom-call(s32[1]{0:T(128)} %bitcast.6.first_r, bf16[256,3200]{1,0:T(8,128)(2,1)} %copy-done, bf16[256,3200]{1,0:T(8,128)(2,1)} %collective-permute-done.6.refs_1_, bf16[2,1152,3072]{2,1,0:T(8,128)(2,1)} %refs_2_.3, bf16[2,1152,3072]{2,1,0:T(8,128)(2,1)} %refs_3_.3, ...), custom_call_target="tpu_custom_call" | custom-call | tf_op jit(solution)/shard_map/pallas_call | solution.py:266
  130.1 0.5 collective-permute-start.7
  130.6 0.1 reshape.214
  130.7 0.6 fusion.4
  131.3 0.2 copy-done.4
  131.5 2.1 add_convert_fusion.1
  133.6 1.8 collective-permute-start.14
  135.4 2.0 add_convert_fusion.3
  137.3 0.3 collective-permute-start.8
  137.7 5.0 %collective-permute-start.2 = (bf16[17,128,128]{2,1,0:T(8,128)(2,1)S(1)}, bf16[17,128,128]{2,1,0:T(8,128)(2,1)S(1)}, u32[]{:S(2)}, u32[]{:S(2)}) collective-permute-start(bf16[17,128,128]{2,1,0:T(8,128)(2,1)S(1)} %pad_maximum_fusion.4), channel_id=1, source_target_pairs={{0,16},{1,17},{2,18},{3,19},{4,20},{5,21},{6,22},{7,23},{8,24},{9,... | collective-permute-start | bytes 1671176 | tf_op jit(solution)/shard_map/ppermute | solution.py:71
  142.7 4.2 %collective-permute-done.14 = bf16[128,3072]{1,0:T(8,128)(2,1)S(1)} collective-permute-done((bf16[128,3072]{1,0:T(8,128)(2,1)S(1)}, bf16[128,3072]{1,0:T(8,128)(2,1)S(1)}, u32[]{:S(2)}, u32[]{:S(2)}) %collective-permute-start.14) | collective-permute-done | bytes 786464 | tf_op jit(solution)/shard_map/ppermute | solution.py:71
  146.8 0.2 add_convert_fusion.5
  147.0 8.7 %collective-permute-start.15 = (bf16[64,3072]{1,0:T(8,128)(2,1)S(1)}, bf16[64,3072]{1,0:T(8,128)(2,1)S(1)}, u32[]{:S(2)}, u32[]{:S(2)}) collective-permute-start(bf16[64,3072]{1,0:T(8,128)(2,1)S(1)} %get-tuple-element.40), channel_id=1, source_target_pairs={{0,8},{1,17},{2,10},{3,19},{4,12},{5,21},{6,14},{7,23},{8,0},{9,25... | collective-permute-start | bytes 1179656 | tf_op jit(solution)/shard_map/ppermute | solution.py:71
  155.7 21.1 %collective-permute-done.8 = bf16[128,3072]{1,0:T(8,128)(2,1)S(1)} collective-permute-done((bf16[128,3072]{1,0:T(8,128)(2,1)S(1)}, bf16[128,3072]{1,0:T(8,128)(2,1)S(1)}, u32[]{:S(2)}, u32[]{:S(2)}) %collective-permute-start.8) | collective-permute-done | bytes 786464 | tf_op jit(solution)/shard_map/ppermute | solution.py:71
  176.8 0.2 add_convert_fusion.7
  177.0 4.3 %collective-permute-start.9 = (bf16[64,3072]{1,0:T(8,128)(2,1)S(1)}, bf16[64,3072]{1,0:T(8,128)(2,1)S(1)}, u32[]{:S(2)}, u32[]{:S(2)}) collective-permute-start(bf16[64,3072]{1,0:T(8,128)(2,1)S(1)} %get-tuple-element.38), channel_id=1, source_target_pairs={{0,8},{1,17},{2,10},{3,19},{4,12},{5,21},{6,14},{7,23},{8,0},{9,25... | collective-permute-start | bytes 1179656 | tf_op jit(solution)/shard_map/ppermute | solution.py:71
  181.4 1.3 collective-permute-start.16
  182.7 16.9 %collective-permute-done.9 = bf16[64,3072]{1,0:T(8,128)(2,1)S(1)} collective-permute-done((bf16[64,3072]{1,0:T(8,128)(2,1)S(1)}, bf16[64,3072]{1,0:T(8,128)(2,1)S(1)}, u32[]{:S(2)}, u32[]{:S(2)}) %collective-permute-start.9) | collective-permute-done | bytes 393248 | tf_op jit(solution)/shard_map/ppermute | solution.py:71
  199.7 1.3 collective-permute-start.10
  201.1 1.3 collective-permute-start.17
  202.4 1.5 add_select_fusion
  203.8 7.1 %shard_map.147 = (bf16[128,1024]{1,0:T(8,128)(2,1)}, bf16[128,1024]{1,0:T(8,128)(2,1)}, bf16[128,1024]{1,0:T(8,128)(2,1)}, bf16[128,1024]{1,0:T(8,128)(2,1)}) custom-call(bf16[128,1024]{1,0:T(8,128)(2,1)} %q_r.3, bf16[128,1024]{1,0:T(8,128)(2,1)} %k_r.3, bf16[128,1024]{1,0:T(8,128)(2,1)} %v_r.3, bf16[128,1024]{1,0:T(8,128)(2,1)} %d_r.3, ...), custom_call_target="tpu_custom_call" | custom-call | tf_op jit(solution)/shard_map/pallas_call | solution.py:147
  210.9 0.8 add_convert_fusion.8
  (52 shorter events, 0.9 us)
Async XLA Ops:
  0.6 34.1 %copy-start.1 = (bf16[32,3072]{1,0:T(8,128)(2,1)S(1)}, bf16[32,3072]{1,0:T(8,128)(2,1)}, u32[]{:S(2)}) copy-start(bf16[32,3072]{1,0:T(8,128)(2,1)} %param.16) | copy-start | bytes 589828
  3.2 5.6 %collective-permute-start.3 = (bf16[32,3200]{1,0:T(8,128)(2,1)S(1)}, bf16[32,3200]{1,0:T(8,128)(2,1)S(1)}, u32[]{:S(2)}, u32[]{:S(2)}) collective-permute-start(bf16[32,3200]{1,0:T(8,128)(2,1)S(1)} %pad_maximum_fusion.6), channel_id=1, source_target_pairs={{0,16},{1,5},{2,18},{3,7},{4,20},{5,1},{6,22},{7,3},{8,24},{9,13},... | collective-permute-start | bytes 614408 | tf_op jit(solution)/shard_map/ppermute | solution.py:71
  9.7 12.4 %collective-permute-start.4 = (bf16[64,3200]{1,0:T(8,128)(2,1)S(1)}, bf16[64,3200]{1,0:T(8,128)(2,1)S(1)}, u32[]{:S(2)}, u32[]{:S(2)}) collective-permute-start(bf16[64,3200]{1,0:T(8,128)(2,1)S(1)} %pad_maximum_fusion.5), channel_id=1, source_target_pairs={{0,8},{1,17},{2,10},{3,19},{4,12},{5,21},{6,14},{7,23},{8,0},{9,25... | collective-permute-start | bytes 1228808 | tf_op jit(solution)/shard_map/ppermute | solution.py:71
  23.1 13.0 %copy-start.6 = (f32[128,8]{0,1:T(8,128)S(1)}, f32[128,8]{0,1:T(8,128)}, u32[]{:S(2)}) copy-start(f32[128,8]{0,1:T(8,128)} %param.15) | copy-start | bytes 12292
  23.2 11.6 %collective-permute-start.5 = (bf16[128,3200]{1,0:T(8,128)(2,1)S(1)}, bf16[128,3200]{1,0:T(8,128)(2,1)S(1)}, u32[]{:S(2)}, u32[]{:S(2)}) collective-permute-start(bf16[128,3200]{1,0:T(8,128)(2,1)S(1)} %pad_maximum_fusion.1), channel_id=1, source_target_pairs={{0,2},{1,9},{2,0},{3,11},{4,6},{5,13},{6,4},{7,15},{8,10},{9,1},{1... | collective-permute-start | bytes 2457608 | tf_op jit(solution)/shard_map/ppermute | solution.py:71
  34.8 40.1 %copy-start = (bf16[256,3200]{1,0:T(8,128)(2,1)}, bf16[256,3200]{1,0:T(8,128)(2,1)S(1)}, u32[]{:S(2)}) copy-start(bf16[256,3200]{1,0:T(8,128)(2,1)S(1)} %pad_maximum_fusion.refs_0_) | copy-start | bytes 4915204
  34.9 21.3 %collective-permute-start.11 = (bf16[256,3200]{1,0:T(8,128)(2,1)S(1)}, bf16[256,3200]{1,0:T(8,128)(2,1)}, u32[]{:S(2)}, u32[]{:S(2)}) collective-permute-start(bf16[256,3200]{1,0:T(8,128)(2,1)S(1)} %pad_maximum_fusion.refs_0_), channel_id=1, source_target_pairs={{0,4},{1,3},{2,6},{3,1},{4,0},{5,7},{6,2},{7,5},{8,12},{9,11},{10,... | collective-permute-start | bytes 4915208 | tf_op jit(solution)/shard_map/ppermute | solution.py:71
  44.4 23.0 %collective-permute-start = (bf16[17,128,128]{2,1,0:T(8,128)(2,1)S(1)}, bf16[17,128,128]{2,1,0:T(8,128)(2,1)S(1)}, u32[]{:S(2)}, u32[]{:S(2)}) collective-permute-start(bf16[17,128,128]{2,1,0:T(8,128)(2,1)S(1)} %pad_maximum_fusion.2), channel_id=1, source_target_pairs={{0,4},{1,5},{2,6},{3,7},{4,0},{5,1},{6,2},{7,3},{8,12},{9,13},{10,... | collective-permute-start | bytes 1671176 | tf_op jit(solution)/shard_map/ppermute | solution.py:71
  56.2 19.7 %collective-permute-start.12 = (bf16[256,3200]{1,0:T(8,128)(2,1)}, bf16[256,3200]{1,0:T(8,128)(2,1)}, u32[]{:S(2)}, u32[]{:S(2)}) collective-permute-start(bf16[256,3200]{1,0:T(8,128)(2,1)} %collective-permute-done.11.refs_0_), channel_id=1, source_target_pairs={{0,1},{1,0},{2,3},{3,2},{4,5},{5,4},{6,7},{7,6},{8,9},{9,8},{10,11... | collective-permute-start | bytes 4915208 | tf_op jit(solution)/shard_map/ppermute | solution.py:71
  67.5 35.4 %collective-permute-start.6 = (bf16[256,3200]{1,0:T(8,128)(2,1)S(1)}, bf16[256,3200]{1,0:T(8,128)(2,1)}, u32[]{:S(2)}, u32[]{:S(2)}) collective-permute-start(bf16[256,3200]{1,0:T(8,128)(2,1)S(1)} %pad_maximum_fusion.refs_0_), channel_id=1, source_target_pairs={{0,1},{1,0},{2,3},{3,2},{4,5},{5,4},{6,7},{7,6},{8,9},{9,8},{10,11... | collective-permute-start | bytes 4915208 | tf_op jit(solution)/shard_map/ppermute | solution.py:71
  75.8 27.0 %collective-permute-start.1 = (bf16[17,128,128]{2,1,0:T(8,128)(2,1)}, bf16[17,128,128]{2,1,0:T(8,128)(2,1)S(1)}, u32[]{:S(2)}, u32[]{:S(2)}) collective-permute-start(bf16[17,128,128]{2,1,0:T(8,128)(2,1)} %pad_maximum_fusion.3), channel_id=1, source_target_pairs={{0,8},{1,9},{2,10},{3,11},{4,12},{5,13},{6,14},{7,15},{8,0},{9,1},... | collective-permute-start | bytes 1671176 | tf_op jit(solution)/shard_map/ppermute | solution.py:71
  102.8 28.6 %collective-permute-start.13 = (bf16[256,3072]{1,0:T(8,128)(2,1)}, bf16[256,3072]{1,0:T(8,128)(2,1)}, u32[]{:S(2)}, u32[]{:S(2)}) collective-permute-start(bf16[256,3072]{1,0:T(8,128)(2,1)} %get-tuple-element.24), channel_id=1, source_target_pairs={{0,1},{1,0},{2,3},{3,2},{4,5},{5,4},{6,7},{7,6},{8,9},{9,8},{10,11... | collective-permute-start | bytes 4718600 | tf_op jit(solution)/shard_map/ppermute | solution.py:71
  102.9 27.8 %copy-start.2 = (bf16[8,128,128]{2,1,0:T(8,128)(2,1)S(1)}, bf16[8,128,128]{2,1,0:T(8,128)(2,1)}, u32[]{:S(2)}) copy-start(bf16[8,128,128]{2,1,0:T(8,128)(2,1)} %get-tuple-element.15) | copy-start | bytes 786436
  102.9 27.8 %copy-start.3 = (bf16[8,128,128]{2,1,0:T(8,128)(2,1)S(1)}, bf16[8,128,128]{2,1,0:T(8,128)(2,1)}, u32[]{:S(2)}) copy-start(bf16[8,128,128]{2,1,0:T(8,128)(2,1)} %get-tuple-element.16) | copy-start | bytes 786436
  130.1 1.4 copy-start.4
  130.1 5.3 %collective-permute-start.7 = (bf16[256,3072]{1,0:T(8,128)(2,1)}, bf16[256,3072]{1,0:T(8,128)(2,1)}, u32[]{:S(2)}, u32[]{:S(2)}) collective-permute-start(bf16[256,3072]{1,0:T(8,128)(2,1)} %get-tuple-element.22), channel_id=1, source_target_pairs={{0,1},{1,0},{2,3},{3,2},{4,5},{5,4},{6,7},{7,6},{8,9},{9,8},{10,11... | collective-permute-start | bytes 4718600 | tf_op jit(solution)/shard_map/ppermute | solution.py:71
  131.5 3.9 %copy-start.5 = (bf16[256,3072]{1,0:T(8,128)(2,1)S(1)}, bf16[256,3072]{1,0:T(8,128)(2,1)}, u32[]{:S(2)}) copy-start(bf16[256,3072]{1,0:T(8,128)(2,1)} %get-tuple-element.21) | copy-start | bytes 4718596
  133.6 13.3 %collective-permute-start.14 = (bf16[128,3072]{1,0:T(8,128)(2,1)S(1)}, bf16[128,3072]{1,0:T(8,128)(2,1)S(1)}, u32[]{:S(2)}, u32[]{:S(2)}) collective-permute-start(bf16[128,3072]{1,0:T(8,128)(2,1)S(1)} %get-tuple-element.34), channel_id=1, source_target_pairs={{0,2},{1,9},{2,0},{3,11},{4,6},{5,13},{6,4},{7,15},{8,10},{9,1},{1... | collective-permute-start | bytes 2359304 | tf_op jit(solution)/shard_map/ppermute | solution.py:71
  137.3 39.5 %collective-permute-start.8 = (bf16[128,3072]{1,0:T(8,128)(2,1)S(1)}, bf16[128,3072]{1,0:T(8,128)(2,1)S(1)}, u32[]{:S(2)}, u32[]{:S(2)}) collective-permute-start(bf16[128,3072]{1,0:T(8,128)(2,1)S(1)} %get-tuple-element.32), channel_id=1, source_target_pairs={{0,2},{1,9},{2,0},{3,11},{4,6},{5,13},{6,4},{7,15},{8,10},{9,1},{1... | collective-permute-start | bytes 2359304 | tf_op jit(solution)/shard_map/ppermute | solution.py:71
  137.7 64.7 %collective-permute-start.2 = (bf16[17,128,128]{2,1,0:T(8,128)(2,1)S(1)}, bf16[17,128,128]{2,1,0:T(8,128)(2,1)S(1)}, u32[]{:S(2)}, u32[]{:S(2)}) collective-permute-start(bf16[17,128,128]{2,1,0:T(8,128)(2,1)S(1)} %pad_maximum_fusion.4), channel_id=1, source_target_pairs={{0,16},{1,17},{2,18},{3,19},{4,20},{5,21},{6,22},{7,23},{8,24},{9,... | collective-permute-start | bytes 1671176 | tf_op jit(solution)/shard_map/ppermute | solution.py:71
  147.0 34.3 %collective-permute-start.15 = (bf16[64,3072]{1,0:T(8,128)(2,1)S(1)}, bf16[64,3072]{1,0:T(8,128)(2,1)S(1)}, u32[]{:S(2)}, u32[]{:S(2)}) collective-permute-start(bf16[64,3072]{1,0:T(8,128)(2,1)S(1)} %get-tuple-element.40), channel_id=1, source_target_pairs={{0,8},{1,17},{2,10},{3,19},{4,12},{5,21},{6,14},{7,23},{8,0},{9,25... | collective-permute-start | bytes 1179656 | tf_op jit(solution)/shard_map/ppermute | solution.py:71
  177.0 22.6 %collective-permute-start.9 = (bf16[64,3072]{1,0:T(8,128)(2,1)S(1)}, bf16[64,3072]{1,0:T(8,128)(2,1)S(1)}, u32[]{:S(2)}, u32[]{:S(2)}) collective-permute-start(bf16[64,3072]{1,0:T(8,128)(2,1)S(1)} %get-tuple-element.38), channel_id=1, source_target_pairs={{0,8},{1,17},{2,10},{3,19},{4,12},{5,21},{6,14},{7,23},{8,0},{9,25... | collective-permute-start | bytes 1179656 | tf_op jit(solution)/shard_map/ppermute | solution.py:71
  181.4 19.6 %collective-permute-start.16 = (bf16[32,3072]{1,0:T(8,128)(2,1)S(1)}, bf16[32,3072]{1,0:T(8,128)(2,1)S(1)}, u32[]{:S(2)}, u32[]{:S(2)}) collective-permute-start(bf16[32,3072]{1,0:T(8,128)(2,1)S(1)} %add_convert_fusion.10), channel_id=1, source_target_pairs={{0,16},{1,5},{2,18},{3,7},{4,20},{5,1},{6,22},{7,3},{8,24},{9,13},... | collective-permute-start | bytes 589832 | tf_op jit(solution)/shard_map/ppermute | solution.py:71
  199.7 11.2 %collective-permute-start.10 = (bf16[32,3072]{1,0:T(8,128)(2,1)S(1)}, bf16[32,3072]{1,0:T(8,128)(2,1)S(1)}, u32[]{:S(2)}, u32[]{:S(2)}) collective-permute-start(bf16[32,3072]{1,0:T(8,128)(2,1)S(1)} %add_convert_fusion.13), channel_id=1, source_target_pairs={{0,16},{1,5},{2,18},{3,7},{4,20},{5,1},{6,22},{7,3},{8,24},{9,13},... | collective-permute-start | bytes 589832 | tf_op jit(solution)/shard_map/ppermute | solution.py:71
  201.1 9.8 %collective-permute-start.17 = (bf16[32,3072]{1,0:T(8,128)(2,1)S(1)}, bf16[32,3072]{1,0:T(8,128)(2,1)S(1)}, u32[]{:S(2)}, u32[]{:S(2)}) collective-permute-start(bf16[32,3072]{1,0:T(8,128)(2,1)S(1)} %add_convert_fusion.9), channel_id=1, source_target_pairs={{0,4},{1,3},{2,6},{3,1},{4,0},{5,7},{6,2},{7,5},{8,12},{9,11},{10,... | collective-permute-start | bytes 589832 | tf_op jit(solution)/shard_map/ppermute | solution.py:71
